TPU v7x, 32 devices: a whole 2x2x4 slice. The times are simulated.
32 devices in a mesh: tower: 2 (over core), dp: 16 (over z, y, x).
Axes of the slice: x: 2, y: 2, z: 4, core: 2. Of those that a mesh axis runs over, the one named last changes fastest.
Arguments:
- tokens: bfloat16 [2, 8192, 768], P('tower', 'dp'), may hold values from -6 to 6
- doc_ids: int32 [2, 8192], P('tower', 'dp'), may hold values from 0 to 11, as said below
- pad_mask: int32 [2, 8192], P('tower', 'dp'), may hold values 0 or 1
- targets: int32 [12], replicated, may hold values from 0 to 11, each once
- w_qkv: bfloat16 [768, 2304], replicated, may hold values from -0.21875 to 0.21875
- w_out: bfloat16 [768, 768], replicated, may hold values from -0.875 to 0.875
- ln1_gain: float32 [768], replicated, may hold values from 0.5 to 1.5
- ln1_bias: float32 [768], replicated, may hold values from -0.6 to 0.6
- w_gate: bfloat16 [768, 3072], replicated, may hold values from -0.21875 to 0.21875
- w_up: bfloat16 [768, 3072], replicated, may hold values from -0.21875 to 0.21875
- w_down: bfloat16 [3072, 768], replicated, may hold values from -0.109375 to 0.109375
- ln2_gain: float32 [768], replicated, may hold values from 0.5 to 1.5
- ln2_bias: float32 [768], replicated, may hold values from -0.6 to 0.6
Outputs:
- scores: float32 [12, 12], replicated
- loss: float32 [], replicated
- token_grad: float32 [2, 8192, 768], P('tower', 'dp')
- w_qkv_grad: float32 [768, 2304], P('dp')
- w_out_grad: float32 [768, 768], P('dp')
- ln1_gain_grad: float32 [768], P('dp')
- ln1_bias_grad: float32 [768], P('dp')
- w_gate_grad: float32 [768, 3072], P('dp')
- w_up_grad: float32 [768, 3072], P('dp')
- w_down_grad: float32 [3072, 768], P('dp')
- ln2_gain_grad: float32 [768], P('dp')
- ln2_bias_grad: float32 [768], P('dp')
Inputs may be any that keep to these rules, and one draw needn't show every extreme that they name: `doc_ids`: within each tower the ids never fall; the k-th aligned group of 2048 slots holds exactly the documents k * 3 to k * 3 + 2, one of them exactly 1024 slots long. `targets`: each document of the second tower is the target of exactly one query.
All inputs are finite; a program needn't handle non-finite values. No bound on the sum of `pad_mask` on one device may be relied on, other than what follows from the above.
Results may differ from a plain program's by a relative error of at most 0.015.
Values may be sent and summed in bfloat16 or wider, within the bound.
A program may use at most 192 MiB of HBM per device.

v0:
```python
import jax
import jax.numpy as jnp
from jax import lax
from jax.sharding import PartitionSpec as P

HEADS = 12
HEAD_DIM = 64
SPAN = 4
DOCS_GRP = 3
precise = lax.Precision.HIGHEST
norm_eps = 1e-05


def swapped(value, axis, bit):
    return lax.ppermute(value, axis, [(i, i ^ 1 << bit) for i in range(lax.axis_size(axis))])


def for_sending(value):
    return jax.tree.map(lambda a: a.astype(jnp.bfloat16) if a.dtype == jnp.float32 else a, value)


def angles_for(positions, half):
    freqs = 1000.0 ** (-jnp.arange(half, dtype=jnp.float32) / half)
    theta = positions.astype(jnp.float32)[:, None] * freqs[None, :]
    return (jnp.cos(theta)[:, None, :], jnp.sin(theta)[:, None, :])


def rotate(values, cosine, sine):
    half = values.shape[-1] // 2
    upper = values[..., :half]
    lower = values[..., half:]
    return jnp.concatenate([upper * cosine - lower * sine, lower * cosine + upper * sine], -1)


def unrotate(values, cosine, sine):
    half = values.shape[-1] // 2
    upper = values[..., :half]
    lower = values[..., half:]
    return jnp.concatenate([upper * cosine + lower * sine, lower * cosine - upper * sine], -1)


def norm_rows(values, gain, bias):
    centred = values - jnp.mean(values, -1, keepdims=True)
    spread = jnp.mean(centred * centred, -1, keepdims=True)
    scale = lax.rsqrt(spread + norm_eps)
    normed = centred * scale
    return (normed * gain + bias, normed, scale)


def norm_back(grad, normed, scale, gain):
    shaped = grad * gain
    inner = (
        shaped
        - jnp.mean(shaped, -1, keepdims=True)
        - normed * jnp.mean(shaped * normed, -1, keepdims=True)
    )
    return (inner * scale, jnp.sum(grad * normed, 0), jnp.sum(grad, 0))


def contract_last(left, right):
    return lax.dot_general(
        left, right, (((1,), (1,)), ((), ())), preferred_element_type=jnp.float32
    )


def contract_first(left, right):
    return lax.dot_general(
        left, right, (((0,), (0,)), ((), ())), preferred_element_type=jnp.float32
    )


def local(
    tokens,
    doc_ids,
    pad_mask,
    targets,
    w_qkv,
    w_out,
    ln1_gain,
    ln1_bias,
    w_gate,
    w_up,
    w_down,
    ln2_gain,
    ln2_bias,
):
    width = w_out.shape[0]
    rows = tokens[0]
    count = rows.shape[0]
    tower = lax.axis_index("tower")
    place = lax.axis_index("dp")
    member_of = doc_ids[0] % DOCS_GRP
    live_row = pad_mask[0] == 1
    positions = place % SPAN * count + jnp.arange(count, dtype=jnp.int32)
    cosine, sine = angles_for(positions, HEAD_DIM // 2)
    mixed = jnp.dot(rows, w_qkv, preferred_element_type=jnp.float32)
    query = rotate(mixed[:, :width].reshape(count, HEADS, HEAD_DIM), cosine, sine).astype(
        jnp.bfloat16
    )
    keys = rotate(mixed[:, width : 2 * width].reshape(count, HEADS, HEAD_DIM), cosine, sine).astype(
        jnp.bfloat16
    )
    values = mixed[:, 2 * width :].astype(jnp.bfloat16)
    key_tags = jnp.where(live_row, member_of, -1).astype(jnp.bfloat16)
    group_keys = keys.reshape(count, width)
    group_values = values
    group_tags = key_tags
    levels = SPAN.bit_length() - 1
    for level in range(levels):
        other = swapped((group_keys, group_values, group_tags), "dp", level)
        group_keys = jnp.concatenate([group_keys, other[0]], 0)
        group_values = jnp.concatenate([group_values, other[1]], 0)
        group_tags = jnp.concatenate([group_tags, other[2]], 0)
    group_len = group_keys.shape[0]
    key_tag = group_tags.astype(jnp.float32)
    keys_heads = group_keys.reshape(group_len, HEADS, HEAD_DIM).transpose(1, 0, 2)
    values_heads = group_values.reshape(group_len, HEADS, HEAD_DIM).transpose(1, 0, 2)
    block = min(512, count)
    nblocks = count // block
    query_heads = query.transpose(1, 0, 2).reshape(HEADS, nblocks, block, HEAD_DIM)
    query_tag = member_of.astype(jnp.float32).reshape(nblocks, block)

    def head_scores(query_block, tag_block, head_keys):
        scores = contract_last(query_block, head_keys) * 0.125
        return jnp.where(tag_block[:, None] == key_tag[None, :], scores, -1e30)

    def attend_head(parts):
        head_query, head_keys, head_values = parts

        def attend_block(inputs):
            query_block, tag_block = inputs
            masked = head_scores(query_block, tag_block, head_keys)
            top = jnp.max(masked, -1, keepdims=True)
            expo = jnp.exp(masked - top)
            total = jnp.sum(expo, -1, keepdims=True)
            probs = (expo / total).astype(jnp.bfloat16)
            result = jnp.dot(probs, head_values, preferred_element_type=jnp.float32)
            return (result, (top + jnp.log(total))[:, 0])

        return lax.map(attend_block, (head_query, query_tag))

    outputs, log_totals = lax.map(attend_head, (query_heads, keys_heads, values_heads))
    attended = outputs.transpose(1, 2, 0, 3).reshape(count, width).astype(jnp.bfloat16)
    branch = jnp.dot(attended, w_out, preferred_element_type=jnp.float32)
    first, normed_one, scale_one = norm_rows(rows.astype(jnp.float32) + branch, ln1_gain, ln1_bias)
    inner = first.astype(jnp.bfloat16)
    gate = jnp.dot(inner, w_gate, preferred_element_type=jnp.float32)
    upper = jnp.dot(inner, w_up, preferred_element_type=jnp.float32)
    sigmoid = jax.nn.sigmoid(gate)
    activated = jax.nn.silu(gate)
    hidden = (activated * upper).astype(jnp.bfloat16)
    second, normed_two, scale_two = norm_rows(
        first + jnp.dot(hidden, w_down, preferred_element_type=jnp.float32), ln2_gain, ln2_bias
    )
    member = ((member_of[:, None] == jnp.arange(DOCS_GRP)[None, :]) & live_row[:, None]).astype(
        jnp.float32
    )
    sums = jnp.dot(member.T, second, precision=precise)
    group = place // SPAN
    part_sums = lax.all_gather(sums, "dp", axis=0, tiled=True)
    own_pooled = jnp.sum(part_sums.reshape(-1, SPAN, DOCS_GRP, width), 1).reshape(-1, width)
    own_embed = own_pooled * lax.rsqrt(jnp.sum(own_pooled * own_pooled, -1, keepdims=True) + 1e-06)
    embed = lax.all_gather(
        own_embed[None].astype(jnp.bfloat16), "tower", axis=0, tiled=True
    ).astype(jnp.float32)
    scores = jnp.dot(embed[0], embed[1].T, precision=precise) * 50.0
    docs = scores.shape[0]
    top = jnp.max(scores, -1, keepdims=True)
    log_sums = top[:, 0] + jnp.log(jnp.sum(jnp.exp(scores - top), -1))
    onehot = (jnp.arange(docs)[None, :] == targets[:, None]).astype(jnp.float32)
    chosen = jnp.sum(onehot * scores, -1)
    loss = jnp.mean(log_sums - chosen)
    grad_scores = (jnp.exp(scores - log_sums[:, None]) - onehot) / docs
    grad_query_embed = jnp.dot(grad_scores, embed[1], precision=precise) * 50.0
    grad_doc_embed = jnp.dot(grad_scores.T, embed[0], precision=precise) * 50.0
    own_grad = jnp.where(tower == 0, grad_query_embed, grad_doc_embed)
    start = group * DOCS_GRP
    grad_mine = lax.dynamic_slice_in_dim(own_grad, start, DOCS_GRP, 0)
    pooled_mine = lax.dynamic_slice_in_dim(own_pooled, start, DOCS_GRP, 0)
    inverse = lax.rsqrt(jnp.sum(pooled_mine * pooled_mine, -1, keepdims=True) + 1e-06)
    grad_pool = inverse * grad_mine - inverse**3 * pooled_mine * jnp.sum(
        pooled_mine * grad_mine, -1, keepdims=True
    )
    grad_second = jnp.dot(member, grad_pool, precision=precise)
    grad_h2, gain_two_grad, bias_two_grad = norm_back(grad_second, normed_two, scale_two, ln2_gain)
    grad_mlp = grad_h2.astype(jnp.bfloat16)
    w_down_grad = contract_first(hidden, grad_mlp)
    grad_hidden = contract_last(grad_mlp, w_down)
    grad_gate = (grad_hidden * upper * sigmoid * (1.0 + gate * (1.0 - sigmoid))).astype(
        jnp.bfloat16
    )
    grad_up = (grad_hidden * activated).astype(jnp.bfloat16)
    w_gate_grad = contract_first(inner, grad_gate)
    w_up_grad = contract_first(inner, grad_up)
    grad_first = grad_h2 + contract_last(grad_gate, w_gate) + contract_last(grad_up, w_up)
    grad_h1, gain_one_grad, bias_one_grad = norm_back(grad_first, normed_one, scale_one, ln1_gain)
    grad_branch = grad_h1.astype(jnp.bfloat16)
    w_out_grad = contract_first(attended, grad_branch)
    grad_attended = contract_last(grad_branch, w_out).astype(jnp.bfloat16)
    grad_heads = (
        grad_attended.reshape(count, HEADS, HEAD_DIM)
        .transpose(1, 0, 2)
        .reshape(HEADS, nblocks, block, HEAD_DIM)
    )

    def back_head(parts):
        head_query, head_keys, head_values, head_grad, head_totals = parts

        def back_block(carry, inputs):
            key_acc, value_acc = carry
            query_block, tag_block, grad_block, total_block = inputs
            masked = head_scores(query_block, tag_block, head_keys)
            probs = jnp.exp(masked - total_block[:, None])
            grad_probs = contract_last(grad_block, head_values)
            inner_sum = jnp.sum(probs * grad_probs, -1, keepdims=True)
            grad_logits = (probs * (grad_probs - inner_sum)).astype(jnp.bfloat16)
            grad_query_block = (
                jnp.dot(grad_logits, head_keys, preferred_element_type=jnp.float32) * 0.125
            )
            key_acc = key_acc + contract_first(grad_logits, query_block) * 0.125
            value_acc = value_acc + contract_first(probs.astype(jnp.bfloat16), grad_block)
            return ((key_acc, value_acc), grad_query_block)

        empty = jnp.zeros((group_len, HEAD_DIM), jnp.float32)
        (key_grad, value_grad), query_grad = lax.scan(
            back_block, (empty, empty), (head_query, query_tag, head_grad, head_totals)
        )
        return (key_grad, value_grad, query_grad)

    key_grads, value_grads, query_grads = lax.map(
        back_head, (query_heads, keys_heads, values_heads, grad_heads, log_totals)
    )
    key_full = key_grads.transpose(1, 0, 2).reshape(group_len, width)
    value_full = value_grads.transpose(1, 0, 2).reshape(group_len, width)
    for level in reversed(range(levels)):
        half = key_full.shape[0] // 2
        returned = swapped(
            (for_sending(key_full[half:]), for_sending(value_full[half:])), "dp", level
        )
        key_full = key_full[:half] + returned[0]
        value_full = value_full[:half] + returned[1]
    grad_query_rows = unrotate(
        query_grads.transpose(1, 2, 0, 3).reshape(count, HEADS, HEAD_DIM), cosine, sine
    )
    grad_key_rows = unrotate(key_full.reshape(count, HEADS, HEAD_DIM), cosine, sine)
    grad_mixed = jnp.concatenate(
        [grad_query_rows.reshape(count, width), grad_key_rows.reshape(count, width), value_full], 1
    ).astype(jnp.bfloat16)
    w_qkv_grad = contract_first(rows, grad_mixed)
    token_grad = grad_h1 + contract_last(grad_mixed, w_qkv)
    gain_grads = jnp.stack([gain_one_grad, bias_one_grad, gain_two_grad, bias_two_grad], 1)
    terms = (w_qkv_grad, w_out_grad, w_gate_grad, w_up_grad, w_down_grad, gain_grads)
    pieces = (
        lax.psum_scatter(terms[0], "dp", scatter_dimension=0, tiled=True),
        lax.psum_scatter(terms[1], "dp", scatter_dimension=0, tiled=True),
        lax.psum_scatter(terms[2], "dp", scatter_dimension=0, tiled=True),
        lax.psum_scatter(terms[3], "dp", scatter_dimension=0, tiled=True),
        lax.psum_scatter(terms[4], "dp", scatter_dimension=0, tiled=True),
        lax.psum_scatter(terms[5], "dp", scatter_dimension=0, tiled=True),
    )
    totals = (
        lax.psum(pieces[0].astype(jnp.bfloat16), "tower").astype(jnp.float32),
        lax.psum(pieces[1].astype(jnp.bfloat16), "tower").astype(jnp.float32),
        lax.psum(pieces[2].astype(jnp.bfloat16), "tower").astype(jnp.float32),
        lax.psum(pieces[3].astype(jnp.bfloat16), "tower").astype(jnp.float32),
        lax.psum(pieces[4].astype(jnp.bfloat16), "tower").astype(jnp.float32),
        lax.psum(pieces[5].astype(jnp.bfloat16), "tower").astype(jnp.float32),
    )
    gains_out = totals[5]
    return (
        scores,
        loss,
        token_grad[None],
        totals[0],
        totals[1],
        gains_out[:, 0],
        gains_out[:, 1],
        totals[2],
        totals[3],
        totals[4],
        gains_out[:, 2],
        gains_out[:, 3],
    )


def solution(mesh):
    placed = (
        P("tower", "dp", None),
        P("tower", "dp"),
        P("tower", "dp"),
        P(),
        P(),
        P(),
        P(),
        P(),
        P(),
        P(),
        P(),
        P(),
        P(),
    )
    return jax.shard_map(
        local,
        mesh=mesh,
        in_specs=placed,
        out_specs=(
            P(),
            P(),
            P("tower", "dp", None),
            P("dp", None),
            P("dp", None),
            P("dp"),
            P("dp"),
            P("dp", None),
            P("dp", None),
            P("dp", None),
            P("dp"),
            P("dp"),
        ),
        check_vma=False,
    )
```

profile of v0, /device:TPU:0, one launch (start us, length us, event | category | flops | bytes accessed | tf_op | source)
XLA Modules:
  0.0 1405.6 jit_solution(15379904082017169689)
XLA Ops:
  27.5 9.6 collective-permute-done.4
  41.8 11.2 collective-permute-done.2
  68.5 40.1 %collective-permute-done.1 = bf16[1024]{0:T(1024)(128)(2,1)} collective-permute-done((bf16[1024]{0:T(1024)(128)(2,1)S(1)}, bf16[1024]{0:T(1024)(128)(2,1)}, u32[]{:S(2)}, u32[]{:S(2)}) %collective-permute-start.1) | collective-permute-done | bytes 2080 | tf_op jit(solution)/shard_map/ppermute | solution.py:15
  117.6 6.6 copy.55
  128.1 6.6 copy.54
  134.7 71.9 %while.28 = (s32[]{:T(128)}, bf16[12,1,512,64]{2,3,1,0:T(8,128)(2,1)}, f32[12,1,512]{2,1,0:T(1,128)}, f32[1,512]{1,0:T(1,128)S(1)}, f32[2048]{0:T(1024)S(1)}, /*...) while((s32[]{:T(128)}, ...), condition=%wide.region_3.4_spmd.clone, body=%wide.region_0.3_spmd.sunk.clone | while | flops 277872128 | bytes 13926497 | solution.py:142
  210.1 5.1 fusion.98
  225.2 42.0 %all-gather = f32[16,3,768]{2,1,0:T(4,128)S(1)} all-gather(f32[1,3,768]{2,1,0:T(4,128)S(1)} %fusion.44), channel_id=1, replica_groups=mesh['tower'=2,'dp'=16] {'dp'}, dimensions={0}, use_global_device_ids=true | all-gather | bytes 156672 | tf_op jit(solution)/shard_map/all_gather | solution.py:160
  283.2 9.4 multiply_convert_fusion.1
  306.9 149.5 %while.29 = (s32[]{:T(128)}, f32[12,2048,64]{1,2,0:T(8,128)}, f32[12,2048,64]{1,2,0:T(8,128)}, f32[12,1,512,64]{2,3,1,0:T(8,128)}, f32[1,512]{1,0:T(1,128)}, /*i...) while((s32[]{:T(128)}, f32[12,2048,64]{1,2,0:T(8,128)}, ...), condition=%wide.region_22.23_spmd.clone, body=%wide.region_20.22_spmd.sunk.clone | while | flops 681737728 | bytes 34636948 | solution.py:230
  463.4 32.6 %collective-permute-done.6 = bf16[1024,768]{0,1:T(8,128)(2,1)S(1)} collective-permute-done((bf16[1024,768]{0,1:T(8,128)(2,1)S(1)}, bf16[1024,768]{0,1:T(8,128)(2,1)S(1)}, u32[]{:S(2)}, u32[]{:S(2)}) %collective-permute-start.6) | collective-permute-done | bytes 1572896 | tf_op jit(solution)/shard_map/ppermute | solution.py:15
  497.4 31.5 %collective-permute-done.8 = bf16[1024,768]{0,1:T(8,128)(2,1)S(1)} collective-permute-done((bf16[1024,768]{0,1:T(8,128)(2,1)S(1)}, bf16[1024,768]{0,1:T(8,128)(2,1)S(1)}, u32[]{:S(2)}, u32[]{:S(2)}) %collective-permute-start.8) | collective-permute-done | bytes 1572896 | tf_op jit(solution)/shard_map/ppermute | solution.py:15
  531.9 16.9 %collective-permute-done.9 = bf16[512,768]{0,1:T(8,128)(2,1)S(1)} collective-permute-done((bf16[512,768]{0,1:T(8,128)(2,1)S(1)}, bf16[512,768]{0,1:T(8,128)(2,1)S(1)}, u32[]{:S(2)}, u32[]{:S(2)}) %collective-permute-start.9) | collective-permute-done | bytes 786464 | tf_op jit(solution)/shard_map/ppermute | solution.py:15
  554.8 8.0 copy.64
  563.2 8.7 fusion.57
  571.9 8.4 fusion.101
  580.4 8.6 fusion.100
  595.0 115.7 %reduce-scatter.19.cloned.1.call-done = f32[48,2304]{1,0:T(8,128)} async-done(((f32[768,2304]{1,0:T(8,128)}), f32[48,2304]{1,0:T(8,128)}) %reduce-scatter.19.cloned.1.call-update) | async-done | bytes 442384
  712.7 174.4 %reduce-scatter.17.cloned.1.call-done = f32[192,768]{1,0:T(8,128)} async-done(((f32[3072,768]{1,0:T(8,128)}), f32[192,768]{1,0:T(8,128)}) %reduce-scatter.17.cloned.1.call-update) | async-done | bytes 589840 | tf_op jit(solution)/shard_map/reduce_scatter | solution.py:258
  888.9 173.7 %reduce-scatter.15.cloned.1.call-done = f32[48,3072]{1,0:T(8,128)} async-done(((f32[768,3072]{1,0:T(8,128)}), f32[48,3072]{1,0:T(8,128)}) %reduce-scatter.15.cloned.1.call-update) | async-done | bytes 589840 | tf_op jit(solution)/shard_map/reduce_scatter | solution.py:257
  1064.4 174.7 %reduce-scatter.13.cloned.1.call-done = f32[48,3072]{1,0:T(8,128)} async-done(((f32[768,3072]{1,0:T(8,128)}), f32[48,3072]{1,0:T(8,128)}) %reduce-scatter.13.cloned.1.call-update) | async-done | bytes 589840 | tf_op jit(solution)/shard_map/reduce_scatter | solution.py:256
  1242.3 122.2 %reduce-scatter.21.cloned.1.call-done = f32[48,4]{1,0:T(8,128)} async-done(((f32[768,4]{1,0:T(8,128)}), f32[48,4]{1,0:T(8,128)}) %reduce-scatter.21.cloned.1.call-update) | async-done | bytes 784
  1368.3 5.3 add_bitcast_fusion
  1373.6 14.7 %all-reduce.3.cloned.1.call-done = (bf16[48,2304]{0,1:T(8,128)(2,1)}, bf16[48,768]{1,0:T(8,128)(2,1)}, bf16[48,3072]{1,0:T(8,128)(2,1)}, bf16[48,3072]{1,0:T(8,128)(2,1)}, bf16[192,768]{1,0:T(8,128)(2,1)}) async-done(((bf16[48,2304]{0,1:T(8,128)(2,1)}, bf16[48,768]{1,0:T(8,128)(2,1)}, bf16[48,3072]{1,0:T(8,128)(2,1)}, bf16[48,3072]{1,0:T(8,128)(2,1)}, bf16[192,768]{1,0:T(8,128)(2,1)}), ...) | async-done | bytes 1179664 | tf_op jit(solution)/shard_map/psum | solution.py:262
  (422 shorter events, 362.1 us)
Async XLA Ops:
  7.2 586.3 %reduce-scatter.11.cloned.1.call-start = ((), (), s32[]{:S(2)}) async-start(), calls=%async_computation.6 | async-start | bytes 2506752 | tf_op jit(solution)/shard_map/reduce_scatter | solution.py:255
  15.5 21.6 %collective-permute-start.4 = (bf16[512,768]{1,0:T(8,128)(2,1)}, bf16[512,768]{1,0:T(8,128)(2,1)}, u32[]{:S(2)}, u32[]{:S(2)}) collective-permute-start(bf16[512,768]{1,0:T(8,128)(2,1)} %slice.177), channel_id=1, source_target_pairs={{0,1},{1,0},{2,3},{3,2},{4,5},{5,4},{6,7},{7,6},{8,9},{9,8},{10,11... | collective-permute-start | bytes 2359304 | tf_op jit(solution)/shard_map/ppermute | solution.py:15
  27.4 27.0 %copy-start.4 = (bf16[512,12,64]{0,2,1:T(8,128)(2,1)}, bf16[512,12,64]{0,2,1:T(8,128)(2,1)S(1)}, u32[]{:S(2)}) copy-start(bf16[512,12,64]{0,2,1:T(8,128)(2,1)S(1)} %maximum_convert_fusion) | copy-start | bytes 2359300
  27.4 28.8 %copy-start.44 = (s32[1,512]{1,0:T(1,128)S(1)}, s32[1,512]{1,0:T(1,128)}, u32[]{:S(2)}) copy-start(s32[1,512]{1,0:T(1,128)} %param.19) | copy-start | bytes 6148
  27.4 28.8 %copy-start.43 = (s32[1,512]{1,0:T(1,128)S(1)}, s32[1,512]{1,0:T(1,128)}, u32[]{:S(2)}) copy-start(s32[1,512]{1,0:T(1,128)} %param.18) | copy-start | bytes 6148
  27.4 25.6 %collective-permute-start.2 = (bf16[512,768]{0,1:T(8,128)(2,1)S(1)}, bf16[512,768]{0,1:T(8,128)(2,1)S(1)}, u32[]{:S(2)}, u32[]{:S(2)}) collective-permute-start(bf16[512,768]{0,1:T(8,128)(2,1)S(1)} %bitcast.217), channel_id=1, source_target_pairs={{0,1},{1,0},{2,3},{3,2},{4,5},{5,4},{6,7},{7,6},{8,9},{9,8},{10,11... | collective-permute-start | bytes 2359304 | tf_op jit(solution)/shard_map/ppermute | solution.py:15
  39.7 69.5 %collective-permute-start.5 = (bf16[1024,768]{1,0:T(8,128)(2,1)}, bf16[1024,768]{1,0:T(8,128)(2,1)}, u32[]{:S(2)}, u32[]{:S(2)}) collective-permute-start(bf16[1024,768]{1,0:T(8,128)(2,1)} %pad_maximum_fusion.3), channel_id=1, source_target_pairs={{0,2},{1,3},{2,0},{3,1},{4,6},{5,7},{6,4},{7,5},{8,10},{9,11},{10,... | collective-permute-start | bytes 4718600 | tf_op jit(solution)/shard_map/ppermute | solution.py:15
  54.4 69.8 %collective-permute-start.3 = (bf16[1024,768]{0,1:T(8,128)(2,1)}, bf16[1024,768]{0,1:T(8,128)(2,1)}, u32[]{:S(2)}, u32[]{:S(2)}) collective-permute-start(bf16[1024,768]{0,1:T(8,128)(2,1)} %pad_maximum_fusion.2), channel_id=1, source_target_pairs={{0,2},{1,3},{2,0},{3,1},{4,6},{5,7},{6,4},{7,5},{8,10},{9,11},{10,... | collective-permute-start | bytes 4718600 | tf_op jit(solution)/shard_map/ppermute | solution.py:15
  56.9 7.1 collective-permute-start
  64.0 44.6 %collective-permute-start.1 = (bf16[1024]{0:T(1024)(128)(2,1)S(1)}, bf16[1024]{0:T(1024)(128)(2,1)}, u32[]{:S(2)}, u32[]{:S(2)}) collective-permute-start(bf16[1024]{0:T(1024)(128)(2,1)S(1)} %pad_maximum_fusion.9), channel_id=1, source_target_pairs={{0,2},{1,3},{2,0},{3,1},{4,6},{5,7},{6,4},{7,5},{8,10},{9,11},{10,... | collective-permute-start | bytes 6152 | tf_op jit(solution)/shard_map/ppermute | solution.py:15
  223.1 44.1 %copy-start.32 = (f32[512]{0:T(512)}, f32[512]{0:T(512)S(1)}, u32[]{:S(2)}) copy-start(f32[512]{0:T(512)S(1)} %broadcast_multiply_fusion.4) | copy-start | bytes 6148
  223.4 43.8 %copy-start.36 = (f32[512]{0:T(512)}, f32[512]{0:T(512)S(1)}, u32[]{:S(2)}) copy-start(f32[512]{0:T(512)S(1)} %add_rsqrt_fusion.1) | copy-start | bytes 6148
  306.9 403.8 %reduce-scatter.19.cloned.1.call-start = ((), (), s32[]{:S(2)}) async-start(), calls=%async_computation.10 | async-start | bytes 7520256
  458.7 37.3 %collective-permute-start.6 = (bf16[1024,768]{0,1:T(8,128)(2,1)S(1)}, bf16[1024,768]{0,1:T(8,128)(2,1)S(1)}, u32[]{:S(2)}, u32[]{:S(2)}) collective-permute-start(bf16[1024,768]{0,1:T(8,128)(2,1)S(1)} %bitcast.235), channel_id=1, source_target_pairs={{0,2},{1,3},{2,0},{3,1},{4,6},{5,7},{6,4},{7,5},{8,10},{9,11},{10,... | collective-permute-start | bytes 4718600 | tf_op jit(solution)/shard_map/ppermute | solution.py:15
  461.3 67.6 %collective-permute-start.8 = (bf16[1024,768]{0,1:T(8,128)(2,1)S(1)}, bf16[1024,768]{0,1:T(8,128)(2,1)S(1)}, u32[]{:S(2)}, u32[]{:S(2)}) collective-permute-start(bf16[1024,768]{0,1:T(8,128)(2,1)S(1)} %bitcast.234), channel_id=1, source_target_pairs={{0,2},{1,3},{2,0},{3,1},{4,6},{5,7},{6,4},{7,5},{8,10},{9,11},{10,... | collective-permute-start | bytes 4718600 | tf_op jit(solution)/shard_map/ppermute | solution.py:15
  463.0 34.0 %slice-start.2 = ((s8[6291456]{0:T(1024)(128)(4,1)}), s8[4194304]{0:T(1024)(128)(4,1)S(1)}, s32[]{:S(2)}) async-start(s8[6291456]{0:T(1024)(128)(4,1)} %bitcast.225), calls=%async_computation.15 | async-start | bytes 8388608
  463.4 33.6 %slice-start.3 = ((s8[6291456]{0:T(1024)(128)(4,1)}), s8[2097152]{0:T(1024)(128)(4,1)S(1)}, s32[]{:S(2)}) async-start(s8[6291456]{0:T(1024)(128)(4,1)} %bitcast.225), calls=%async_computation.16 | async-start | bytes 4194304
  496.9 33.0 %collective-permute-start.7 = (bf16[512,768]{0,1:T(8,128)(2,1)S(1)}, bf16[512,768]{0,1:T(8,128)(2,1)S(1)}, u32[]{:S(2)}, u32[]{:S(2)}) collective-permute-start(bf16[512,768]{0,1:T(8,128)(2,1)S(1)} %slice.176), channel_id=1, source_target_pairs={{0,1},{1,0},{2,3},{3,2},{4,5},{5,4},{6,7},{7,6},{8,9},{9,8},{10,11... | collective-permute-start | bytes 2359304 | tf_op jit(solution)/shard_map/ppermute | solution.py:15
  529.9 18.8 %collective-permute-start.9 = (bf16[512,768]{0,1:T(8,128)(2,1)S(1)}, bf16[512,768]{0,1:T(8,128)(2,1)S(1)}, u32[]{:S(2)}, u32[]{:S(2)}) collective-permute-start(bf16[512,768]{0,1:T(8,128)(2,1)S(1)} %slice.175), channel_id=1, source_target_pairs={{0,1},{1,0},{2,3},{3,2},{4,5},{5,4},{6,7},{7,6},{8,9},{9,8},{10,11... | collective-permute-start | bytes 2359304 | tf_op jit(solution)/shard_map/ppermute | solution.py:15
  562.9 324.2 %reduce-scatter.17.cloned.1.call-start = ((), (), s32[]{:S(2)}) async-start(), calls=%async_computation.9 | async-start | bytes 10027008 | tf_op jit(solution)/shard_map/reduce_scatter | solution.py:258
  571.9 490.7 %reduce-scatter.15.cloned.1.call-start = ((), (), s32[]{:S(2)}) async-start(), calls=%async_computation.8 | async-start | bytes 10027008 | tf_op jit(solution)/shard_map/reduce_scatter | solution.py:257
  580.4 658.7 %reduce-scatter.13.cloned.1.call-start = ((), (), s32[]{:S(2)}) async-start(), calls=%async_computation.7 | async-start | bytes 10027008 | tf_op jit(solution)/shard_map/reduce_scatter | solution.py:256
  589.0 775.4 %reduce-scatter.21.cloned.1.call-start = ((), (), s32[]{:S(2)}) async-start(), calls=%async_computation.11 | async-start | bytes 417792
  593.4 794.9 %all-reduce.3.cloned.1.call-start = ((), (), s32[]{:S(2)}) async-start(), calls=%async_computation.12 | async-start | bytes 3096576 | tf_op jit(solution)/shard_map/psum | solution.py:262
  (65 other events, 323.5 us)
Sparse Core Ops, SparseCore 0:
  307.0 124.3 reduce-scatter.10
  563.0 147.6 reduce-scatter.18
  717.3 169.7 reduce-scatter.16
  892.6 169.8 reduce-scatter.14
  1069.1 170.0 reduce-scatter.12
  1244.2 120.2 reduce-scatter.20
  1368.5 19.7 all-reduce.2
where the time goes:
time: 1410 us
  waiting for transfers between devices  917 us (65%)
  matrix products  273 us (19%)
  local copies, waits for them, and re-layouts  83.7 us (6%)
  other arithmetic  55.8 us (4%)
  blocking collectives  46.3 us (3%)
  between operations  17.2 us (1%)
    unnamed x9, waiting for transfers between devices  238 us
    reduce_scatter x1, waiting for transfers between devices, local(): lax.psum_scatter(terms[2], 'dp', scatter_dimension=0, tiled=True)  175 us
    reduce_scatter x1, waiting for transfers between devices, local(): lax.psum_scatter(terms[4], 'dp', scatter_dimension=0, tiled=True)  174 us
    reduce_scatter x1, waiting for transfers between devices, local(): lax.psum_scatter(terms[3], 'dp', scatter_dimension=0, tiled=True)  174 us
    ppermute x10, waiting for transfers between devices, swapped(): lax.ppermute(value, axis, [(i, i ^ 1 << bit) for i in range(lax.axis_size...  142 us
    dot_general x41, matrix products, contract_last(): lax.dot_general(left, right, (((1,), (1,)), ((), ())), preferred_element_...  100 us
    dot_general x29, matrix products, contract_first(): lax.dot_general(left, right, (((0,), (0,)), ((), ())), preferred_element_...  85.5 us
    all_gather x1, blocking collectives, local(): part_sums = lax.all_gather(sums, 'dp', axis=0, tiled=True)  42 us
  transfers between devices with their start and end apart: 17, of which 12 were waited for; matrix products, arithmetic and copies ran while one was open for 18% of the time, Pallas kernels for 0%

commit v1 on v0

--- a/solution.py
+++ b/solution.py
@@ -157,7 +157,12 @@
     )
     sums = jnp.dot(member.T, second, precision=precise)
     group = place // SPAN
-    part_sums = lax.all_gather(sums, "dp", axis=0, tiled=True)
+    ring = [sums]
+    for hop in range(15):
+        ring.append(lax.ppermute(ring[-1], "dp", [(dev, (dev + 1) % 16) for dev in range(16)]))
+    part_sums = jnp.roll(
+        jnp.concatenate(ring[::-1], axis=0), (lax.axis_index("dp") + 1) * ring[0].shape[0], axis=0
+    )
     own_pooled = jnp.sum(part_sums.reshape(-1, SPAN, DOCS_GRP, width), 1).reshape(-1, width)
     own_embed = own_pooled * lax.rsqrt(jnp.sum(own_pooled * own_pooled, -1, keepdims=True) + 1e-06)
     embed = lax.all_gather(

time: 1410 us -> 1520 us (1.078)
  waiting for transfers between devices: 917 us -> 1030 us
  blocking collectives: 46.3 us -> 4.28 us
  local copies, waits for them, and re-layouts: 83.7 us -> 123 us
    ppermute x0 -> x15, waiting for transfers between devices: none -> 108 us  [local(): lax.ppermute(ring[-1], 'dp', [(dev, (dev + 1) % 16) for dev in range(16)])]
    all_gather x1 -> x0, blocking collectives: 42 us -> none  [local(): part_sums = lax.all_gather(sums, 'dp', axis=0, tiled=True)]
    concatenate x0 -> x1, local copies, waits for them, and re-layouts: none -> 27.8 us  [local(): jnp.roll(jnp.concatenate(ring[::-1], axis=0), (lax.axis_index('dp') + 1)...]
    unnamed x126 -> x152, local copies, waits for them, and re-layouts: 24.3 us -> 32 us
  transfers between devices with their start and end apart: 17 -> 32, of which waited for: 12 -> 27; matrix products, arithmetic and copies ran while one was open for 18% -> 17% of each run, Pallas kernels for 0% -> 0%
where the time goes in v1:
time: 1520 us; the launch traced here: 1510 us
  waiting for transfers between devices  1030 us (68%)
  matrix products  273 us (18%)
  local copies, waits for them, and re-layouts  123 us (8%)
  other arithmetic  58.2 us (4%)
  between operations  17.2 us (1%)
    unnamed x9, waiting for transfers between devices  238 us
    reduce_scatter x1, waiting for transfers between devices, local(): lax.psum_scatter(terms[2], 'dp', scatter_dimension=0, tiled=True)  174 us
    reduce_scatter x1, waiting for transfers between devices, local(): lax.psum_scatter(terms[4], 'dp', scatter_dimension=0, tiled=True)  174 us
    reduce_scatter x1, waiting for transfers between devices, local(): lax.psum_scatter(terms[3], 'dp', scatter_dimension=0, tiled=True)  174 us
    ppermute x10, waiting for transfers between devices, swapped(): lax.ppermute(value, axis, [(i, i ^ 1 << bit) for i in range(lax.axis_size...  142 us
    ppermute x15, waiting for transfers between devices, local(): lax.ppermute(ring[-1], 'dp', [(dev, (dev + 1) % 16) for dev in range(16)])  108 us
    dot_general x41, matrix products, contract_last(): lax.dot_general(left, right, (((1,), (1,)), ((), ())), preferred_element_...  100 us
    dot_general x29, matrix products, contract_first(): lax.dot_general(left, right, (((0,), (0,)), ((), ())), preferred_element_...  85.4 us
  transfers between devices with their start and end apart: 32, of which 27 were waited for; matrix products, arithmetic and copies ran while one was open for 17% of the time, Pallas kernels for 0%

profile of v1, /device:TPU:0, one launch (start us, length us, event | category | flops | bytes accessed | tf_op | source)
XLA Modules:
  0.0 1514.7 jit_solution(352229151834145395)
XLA Ops:
  27.5 9.6 collective-permute-done.4
  41.8 11.2 collective-permute-done.2
  68.3 40.3 %collective-permute-done.1 = bf16[1024]{0:T(1024)(128)(2,1)} collective-permute-done((bf16[1024]{0:T(1024)(128)(2,1)S(1)}, bf16[1024]{0:T(1024)(128)(2,1)}, u32[]{:S(2)}, u32[]{:S(2)}) %collective-permute-start.1) | collective-permute-done | bytes 2080 | tf_op jit(solution)/shard_map/ppermute | solution.py:15
  134.9 72.1 %while.28 = (s32[]{:T(128)}, bf16[12,1,512,64]{2,3,1,0:T(8,128)(2,1)}, f32[12,1,512]{2,1,0:T(1,128)}, f32[1,512]{1,0:T(1,128)S(1)}, f32[2048]{0:T(1024)S(1)}, /*...) while((s32[]{:T(128)}, ...), condition=%wide.region_3.4_spmd.clone, body=%wide.region_0.3_spmd.sunk.clone | while | flops 277872128 | bytes 13926497 | solution.py:142
  234.1 7.3 collective-permute-done.7
  242.0 7.3 collective-permute-done.8
  328.9 7.4 collective-permute-done.19
  336.4 7.5 collective-permute-done.20
  343.9 27.8 %concatenate.61 = f32[96,768]{1,0:T(8,128)} concatenate(f32[3,768]{1,0:T(4,128)} %collective-permute-done.20, f32[3,768]{1,0:T(4,128)} %collective-permute-done.19, f32[3,768]{1,0:T(4,128)} %copy-done.40, f32[3,768]{1,0:T(4,128)} %copy-done.39, f32[3,768]{1,0:T(4,128)} %copy-done.38, f32[3,768]{1,0:T(4,128)} %copy-done.37, f32[3,768]{1,0:T(4,128)} %copy-done.36, ...), dimensions={0} | concatenate | bytes 589824 | tf_op jit(solution)/shard_map/jit(_roll_dynamic)/concatenate | solution.py:163
  392.5 9.4 multiply_convert_fusion.1
  416.6 149.5 %while.29 = (s32[]{:T(128)}, f32[12,2048,64]{1,2,0:T(8,128)}, f32[12,2048,64]{1,2,0:T(8,128)}, f32[12,1,512,64]{2,3,1,0:T(8,128)}, f32[1,512]{1,0:T(1,128)}, /*i...) while((s32[]{:T(128)}, f32[12,2048,64]{1,2,0:T(8,128)}, ...), condition=%wide.region_22.23_spmd.clone, body=%wide.region_20.22_spmd.sunk.clone | while | flops 681737728 | bytes 34636948 | solution.py:235
  573.1 32.6 %collective-permute-done.21 = bf16[1024,768]{0,1:T(8,128)(2,1)S(1)} collective-permute-done((bf16[1024,768]{0,1:T(8,128)(2,1)S(1)}, bf16[1024,768]{0,1:T(8,128)(2,1)S(1)}, u32[]{:S(2)}, u32[]{:S(2)}) %collective-permute-start.21) | collective-permute-done | bytes 1572896 | tf_op jit(solution)/shard_map/ppermute | solution.py:15
  607.1 31.5 %collective-permute-done.23 = bf16[1024,768]{0,1:T(8,128)(2,1)S(1)} collective-permute-done((bf16[1024,768]{0,1:T(8,128)(2,1)S(1)}, bf16[1024,768]{0,1:T(8,128)(2,1)S(1)}, u32[]{:S(2)}, u32[]{:S(2)}) %collective-permute-start.23) | collective-permute-done | bytes 1572896 | tf_op jit(solution)/shard_map/ppermute | solution.py:15
  641.5 16.9 %collective-permute-done.24 = bf16[512,768]{0,1:T(8,128)(2,1)S(1)} collective-permute-done((bf16[512,768]{0,1:T(8,128)(2,1)S(1)}, bf16[512,768]{0,1:T(8,128)(2,1)S(1)}, u32[]{:S(2)}, u32[]{:S(2)}) %collective-permute-start.24) | collective-permute-done | bytes 786464 | tf_op jit(solution)/shard_map/ppermute | solution.py:15
  664.4 8.0 copy.64
  672.6 8.7 fusion.54
  681.4 8.4 fusion.98
  689.9 8.5 fusion.97
  704.5 115.7 %reduce-scatter.19.cloned.1.call-done = f32[48,2304]{1,0:T(8,128)} async-done(((f32[768,2304]{1,0:T(8,128)}), f32[48,2304]{1,0:T(8,128)}) %reduce-scatter.19.cloned.1.call-update) | async-done | bytes 442384
  822.3 174.4 %reduce-scatter.17.cloned.1.call-done = f32[192,768]{1,0:T(8,128)} async-done(((f32[3072,768]{1,0:T(8,128)}), f32[192,768]{1,0:T(8,128)}) %reduce-scatter.17.cloned.1.call-update) | async-done | bytes 589840 | tf_op jit(solution)/shard_map/reduce_scatter | solution.py:263
  998.5 173.6 %reduce-scatter.15.cloned.1.call-done = f32[48,3072]{1,0:T(8,128)} async-done(((f32[768,3072]{1,0:T(8,128)}), f32[48,3072]{1,0:T(8,128)}) %reduce-scatter.15.cloned.1.call-update) | async-done | bytes 589840 | tf_op jit(solution)/shard_map/reduce_scatter | solution.py:262
  1173.9 174.4 %reduce-scatter.13.cloned.1.call-done = f32[48,3072]{1,0:T(8,128)} async-done(((f32[768,3072]{1,0:T(8,128)}), f32[48,3072]{1,0:T(8,128)}) %reduce-scatter.13.cloned.1.call-update) | async-done | bytes 589840 | tf_op jit(solution)/shard_map/reduce_scatter | solution.py:261
  1351.5 122.2 %reduce-scatter.21.cloned.1.call-done = f32[48,4]{1,0:T(8,128)} async-done(((f32[768,4]{1,0:T(8,128)}), f32[48,4]{1,0:T(8,128)}) %reduce-scatter.21.cloned.1.call-update) | async-done | bytes 784
  1482.8 14.7 all-reduce.3.cloned.1.call-done
  (480 shorter events, 479.8 us)
Async XLA Ops:
  7.2 695.7 %reduce-scatter.11.cloned.1.call-start = ((), (), s32[]{:S(2)}) async-start(), calls=%async_computation.6 | async-start | bytes 2506752 | tf_op jit(solution)/shard_map/reduce_scatter | solution.py:260
  15.5 21.6 %collective-permute-start.4 = (bf16[512,768]{1,0:T(8,128)(2,1)}, bf16[512,768]{1,0:T(8,128)(2,1)}, u32[]{:S(2)}, u32[]{:S(2)}) collective-permute-start(bf16[512,768]{1,0:T(8,128)(2,1)} %slice.177), channel_id=1, source_target_pairs={{0,1},{1,0},{2,3},{3,2},{4,5},{5,4},{6,7},{7,6},{8,9},{9,8},{10,11... | collective-permute-start | bytes 2359304 | tf_op jit(solution)/shard_map/ppermute | solution.py:15
  27.4 25.6 %collective-permute-start.2 = (bf16[512,768]{0,1:T(8,128)(2,1)S(1)}, bf16[512,768]{0,1:T(8,128)(2,1)S(1)}, u32[]{:S(2)}, u32[]{:S(2)}) collective-permute-start(bf16[512,768]{0,1:T(8,128)(2,1)S(1)} %bitcast.213), channel_id=1, source_target_pairs={{0,1},{1,0},{2,3},{3,2},{4,5},{5,4},{6,7},{7,6},{8,9},{9,8},{10,11... | collective-permute-start | bytes 2359304 | tf_op jit(solution)/shard_map/ppermute | solution.py:15
  39.8 69.5 %collective-permute-start.5 = (bf16[1024,768]{1,0:T(8,128)(2,1)}, bf16[1024,768]{1,0:T(8,128)(2,1)}, u32[]{:S(2)}, u32[]{:S(2)}) collective-permute-start(bf16[1024,768]{1,0:T(8,128)(2,1)} %pad_maximum_fusion.3), channel_id=1, source_target_pairs={{0,2},{1,3},{2,0},{3,1},{4,6},{5,7},{6,4},{7,5},{8,10},{9,11},{10,... | collective-permute-start | bytes 4718600 | tf_op jit(solution)/shard_map/ppermute | solution.py:15
  54.6 69.7 %collective-permute-start.3 = (bf16[1024,768]{0,1:T(8,128)(2,1)}, bf16[1024,768]{0,1:T(8,128)(2,1)}, u32[]{:S(2)}, u32[]{:S(2)}) collective-permute-start(bf16[1024,768]{0,1:T(8,128)(2,1)} %pad_maximum_fusion.2), channel_id=1, source_target_pairs={{0,2},{1,3},{2,0},{3,1},{4,6},{5,7},{6,4},{7,5},{8,10},{9,11},{10,... | collective-permute-start | bytes 4718600 | tf_op jit(solution)/shard_map/ppermute | solution.py:15
  64.1 44.4 %collective-permute-start.1 = (bf16[1024]{0:T(1024)(128)(2,1)S(1)}, bf16[1024]{0:T(1024)(128)(2,1)}, u32[]{:S(2)}, u32[]{:S(2)}) collective-permute-start(bf16[1024]{0:T(1024)(128)(2,1)S(1)} %pad_maximum_fusion.9), channel_id=1, source_target_pairs={{0,2},{1,3},{2,0},{3,1},{4,6},{5,7},{6,4},{7,5},{8,10},{9,11},{10,... | collective-permute-start | bytes 6152 | tf_op jit(solution)/shard_map/ppermute | solution.py:15
  226.2 7.3 collective-permute-start.6
  234.1 7.3 collective-permute-start.7
  242.0 7.3 collective-permute-start.8
  249.8 7.3 collective-permute-start.9
  257.7 7.3 collective-permute-start.10
  305.1 7.5 collective-permute-start.16
  328.9 7.4 collective-permute-start.19
  336.3 7.6 collective-permute-start.20
  416.1 404.1 %reduce-scatter.19.cloned.1.call-start = ((), (), s32[]{:S(2)}) async-start(), calls=%async_computation.10 | async-start | bytes 7520256
  568.4 37.3 %collective-permute-start.21 = (bf16[1024,768]{0,1:T(8,128)(2,1)S(1)}, bf16[1024,768]{0,1:T(8,128)(2,1)S(1)}, u32[]{:S(2)}, u32[]{:S(2)}) collective-permute-start(bf16[1024,768]{0,1:T(8,128)(2,1)S(1)} %bitcast.231), channel_id=1, source_target_pairs={{0,2},{1,3},{2,0},{3,1},{4,6},{5,7},{6,4},{7,5},{8,10},{9,11},{10,... | collective-permute-start | bytes 4718600 | tf_op jit(solution)/shard_map/ppermute | solution.py:15
  571.0 67.6 %collective-permute-start.23 = (bf16[1024,768]{0,1:T(8,128)(2,1)S(1)}, bf16[1024,768]{0,1:T(8,128)(2,1)S(1)}, u32[]{:S(2)}, u32[]{:S(2)}) collective-permute-start(bf16[1024,768]{0,1:T(8,128)(2,1)S(1)} %bitcast.230), channel_id=1, source_target_pairs={{0,2},{1,3},{2,0},{3,1},{4,6},{5,7},{6,4},{7,5},{8,10},{9,11},{10,... | collective-permute-start | bytes 4718600 | tf_op jit(solution)/shard_map/ppermute | solution.py:15
  606.6 33.0 %collective-permute-start.22 = (bf16[512,768]{0,1:T(8,128)(2,1)S(1)}, bf16[512,768]{0,1:T(8,128)(2,1)S(1)}, u32[]{:S(2)}, u32[]{:S(2)}) collective-permute-start(bf16[512,768]{0,1:T(8,128)(2,1)S(1)} %slice.176), channel_id=1, source_target_pairs={{0,1},{1,0},{2,3},{3,2},{4,5},{5,4},{6,7},{7,6},{8,9},{9,8},{10,11... | collective-permute-start | bytes 2359304 | tf_op jit(solution)/shard_map/ppermute | solution.py:15
  639.5 18.8 %collective-permute-start.24 = (bf16[512,768]{0,1:T(8,128)(2,1)S(1)}, bf16[512,768]{0,1:T(8,128)(2,1)S(1)}, u32[]{:S(2)}, u32[]{:S(2)}) collective-permute-start(bf16[512,768]{0,1:T(8,128)(2,1)S(1)} %slice.175), channel_id=1, source_target_pairs={{0,1},{1,0},{2,3},{3,2},{4,5},{5,4},{6,7},{7,6},{8,9},{9,8},{10,11... | collective-permute-start | bytes 2359304 | tf_op jit(solution)/shard_map/ppermute | solution.py:15
  672.4 324.3 %reduce-scatter.17.cloned.1.call-start = ((), (), s32[]{:S(2)}) async-start(), calls=%async_computation.9 | async-start | bytes 10027008 | tf_op jit(solution)/shard_map/reduce_scatter | solution.py:263
  681.3 490.8 %reduce-scatter.15.cloned.1.call-start = ((), (), s32[]{:S(2)}) async-start(), calls=%async_computation.8 | async-start | bytes 10027008 | tf_op jit(solution)/shard_map/reduce_scatter | solution.py:262
  689.9 658.5 %reduce-scatter.13.cloned.1.call-start = ((), (), s32[]{:S(2)}) async-start(), calls=%async_computation.7 | async-start | bytes 10027008 | tf_op jit(solution)/shard_map/reduce_scatter | solution.py:261
  698.5 775.2 %reduce-scatter.21.cloned.1.call-start = ((), (), s32[]{:S(2)}) async-start(), calls=%async_computation.11 | async-start | bytes 417792
  702.8 794.7 %all-reduce.3.cloned.1.call-start = ((), (), s32[]{:S(2)}) async-start(), calls=%async_computation.12 | async-start | bytes 3096576 | tf_op jit(solution)/shard_map/psum | solution.py:267
  (93 other events, 766.8 us)
Sparse Core Ops, SparseCore 0:
  416.3 124.3 reduce-scatter.10
  672.5 147.6 reduce-scatter.18
  826.8 169.7 reduce-scatter.16
  1002.2 169.8 reduce-scatter.14
  1178.6 169.7 reduce-scatter.12
  1353.4 120.2 reduce-scatter.20
  1477.8 19.7 all-reduce.2
